TPU v7x, 32 devices: a whole 2x2x4 slice. The times are simulated.
32 devices in a mesh: gx: 8 (over y, x, core), gy: 4 (over z).
Axes of the slice: x: 2, y: 2, z: 4, core: 2. Of those that a mesh axis runs over, the one named last changes fastest.
Arguments:
- particle_count: int32 [8, 256, 1024], P(None, ('gx', 'gy')), may hold values from 0 to 12
- drag_coeff: float32 [8, 256, 1024], P(None, ('gx', 'gy')), may hold values from 0.05 to 2
- particle_velocity: float32 [3, 8, 256, 1024], P(None, None, ('gx', 'gy')), may hold values from -6 to 6
- fluid_velocity: float32 [3, 8, 256, 1024], P(None, None, 'gy', 'gx'), may hold values from -6 to 6
Outputs:
- pressure: float32 [8, 256, 1024], P(None, 'gy', 'gx')
- new_velocity: float32 [3, 8, 256, 1024], P(None, None, ('gx', 'gy'))
- pressure_gradient: float32 [3, 8, 256, 1024], P(None, None, ('gx', 'gy'))
All inputs are finite; a program needn't handle non-finite values.
Results may differ from a plain program's by a relative error of at most 0.00002.
Values sent between devices are 32-bit elements; how exact they have to be, the bound alone decides.
A program may use at most 64 MiB of HBM per device.

v0:
```python
import jax
import jax.numpy as jnp
from jax import lax
from jax.sharding import PartitionSpec as P

SWEEPS = 8
particle_volume = 0.05
time_step = 0.5
viscosity = 0.1


def padded_2(cells, sides, width):
    for axis, dim in sides:
        count = lax.axis_size(axis)
        ends = count - 1
        head = lax.slice_in_dim(cells, 0, width, axis=dim)
        tail = lax.slice_in_dim(cells, cells.shape[dim] - width, cells.shape[dim], axis=dim)
        cells = jnp.concatenate(
            [
                lax.ppermute(tail, axis, [(i, (i + 1) % count) for i in range(ends)]),
                cells,
                lax.ppermute(head, axis, [((i + 1) % count, i) for i in range(ends)]),
            ],
            axis=dim,
        )
    return cells


def pad_depth(values):
    widths = [(0, 0)] * (values.ndim - 3) + [(1, 1), (0, 0), (0, 0)]
    return jnp.pad(values, widths)


def pad_plane(values):
    widths = [(0, 0)] * (values.ndim - 2) + [(1, 1), (1, 1)]
    return jnp.pad(values, widths)


def pad_second(values):
    widths = [(0, 0)] * (values.ndim - 1) + [(1, 1)]
    return jnp.pad(values, widths)


def middle(values):
    return values[..., 1:-1, 1:-1, 1:-1]


def neighbour(values, which):
    if which == 0:
        return values[..., 2:, 1:-1, 1:-1]
    if which == 1:
        return values[..., :-2, 1:-1, 1:-1]
    if which == 2:
        return values[..., 1:-1, 2:, 1:-1]
    if which == 3:
        return values[..., 1:-1, :-2, 1:-1]
    if which == 4:
        return values[..., 1:-1, 1:-1, 2:]
    return values[..., 1:-1, 1:-1, :-2]


def face_weights(voids_wide):
    padded = pad_depth(voids_wide)
    centre = middle(padded)
    weights = jnp.stack([0.5 * (centre + neighbour(padded, which)) for which in range(6)])
    weight_sum = weights[0]
    for which in range(1, 6):
        weight_sum = weight_sum + weights[which]
    return (weights, weight_sum)


def momentum(velocity_wide, weights, voids, drag, drag_force):
    padded = pad_depth(velocity_wide)
    centre = middle(padded)
    diffusion = jnp.zeros_like(centre)
    for which in range(6):
        diffusion = diffusion + weights[which][None] * (neighbour(padded, which) - centre)
    return (voids[None] * centre + time_step * viscosity * diffusion + time_step * drag_force) / (
        voids[None] + time_step * drag[None]
    )


def divergence(flux_wide):
    first = flux_wide[0][:, 2:, 1:-1] - flux_wide[0][:, :-2, 1:-1]
    second = flux_wide[1][:, 1:-1, 2:] - flux_wide[1][:, 1:-1, :-2]
    normal = pad_depth(flux_wide[2])[:, 1:-1, 1:-1]
    third = normal[2:] - normal[:-2]
    return 0.5 * (first + second + third) / time_step


def jacobi_sweep(pressure_wide, weights, weight_sum, source):
    padded = pad_depth(pressure_wide)
    total = weights[0] * neighbour(padded, 0)
    for which in range(1, 6):
        total = total + weights[which] * neighbour(padded, which)
    return (total - source) / weight_sum


def gradient_of(pressure_wide):
    padded = pad_depth(pressure_wide)
    first = 0.5 * (padded[1:-1, 2:, 1:-1] - padded[1:-1, :-2, 1:-1])
    second = 0.5 * (padded[1:-1, 1:-1, 2:] - padded[1:-1, 1:-1, :-2])
    third = 0.5 * (padded[2:, 1:-1, 1:-1] - padded[:-2, 1:-1, 1:-1])
    return jnp.stack([first, second, third])


def order_inward(values, across, along):
    fields, planes, x_rows, y_cols = values.shape
    groups = across // along
    rows_each = x_rows // across
    shaped = values.reshape(fields, planes, along, groups, rows_each, y_cols)
    return jnp.swapaxes(shaped, 2, 3).reshape(fields, planes, x_rows, y_cols)


def order_outward(values, across, along):
    fields, planes, x_rows, y_cols = values.shape
    groups = across // along
    rows_each = x_rows // across
    shaped = values.reshape(fields, planes, groups, along, rows_each, y_cols)
    return jnp.swapaxes(shaped, 2, 3).reshape(fields, planes, x_rows, y_cols)


def to_fluid(fields):
    moved = lax.all_to_all(
        lax.all_to_all(fields, "gx", split_axis=3, concat_axis=2, tiled=True),
        "gy",
        split_axis=2,
        concat_axis=2,
        tiled=True,
    )
    return order_inward(moved, lax.axis_size("gx"), lax.axis_size("gy"))


def to_particles(fields):
    ordered = order_outward(fields, lax.axis_size("gx"), lax.axis_size("gy"))
    return lax.all_to_all(
        lax.all_to_all(ordered, "gy", split_axis=2, concat_axis=2, tiled=True),
        "gx",
        split_axis=2,
        concat_axis=3,
        tiled=True,
    )


def shards(particle_count, drag_coeff, particle_velocity, fluid_velocity):
    voids = 1.0 - particle_count.astype(jnp.float32) * particle_volume
    drag_force = drag_coeff[None] * particle_velocity
    slab_velocity = to_particles(fluid_velocity)
    stacked = jnp.concatenate([slab_velocity, voids[None]], axis=0)
    widened = pad_second(padded_2(stacked, ((("gx", "gy"), 2),), 1))
    weights, weight_sum = face_weights(widened[3])
    predicted = momentum(widened[:3], weights, voids, drag_coeff, drag_force)
    flux = voids[None] * predicted
    flux_first = pad_second(padded_2(flux[0:1], ((("gx", "gy"), 2),), 1))
    flux_wide = jnp.concatenate([flux_first, pad_plane(flux[1:3])], axis=0)
    source = divergence(flux_wide)
    pressure = -source / weight_sum
    for sweep_index in range(SWEEPS - 1):
        pressure_wide = pad_second(padded_2(pressure, ((("gx", "gy"), 1),), 1))
        pressure = jacobi_sweep(pressure_wide, weights, weight_sum, source)
    final_wide = pad_second(padded_2(pressure, ((("gx", "gy"), 1),), 1))
    slopes = gradient_of(final_wide)
    velocity = predicted - time_step * slopes
    pressure_out = to_fluid(pressure[None])[0]
    return (pressure_out, velocity, slopes)


def solution(mesh):
    placed = (
        P(None, ("gx", "gy"), None),
        P(None, ("gx", "gy"), None),
        P(None, None, ("gx", "gy"), None),
        P(None, None, "gy", "gx"),
    )
    return jax.shard_map(
        shards,
        mesh=mesh,
        in_specs=placed,
        out_specs=(
            P(None, "gy", "gx"),
            P(None, None, ("gx", "gy"), None),
            P(None, None, ("gx", "gy"), None),
        ),
        check_vma=False,
    )
```

profile of v0, /device:TPU:0, one launch (start us, length us, event | category | flops | bytes accessed | tf_op | source)
XLA Modules:
  0.0 200.9 jit_solution(16246067221753685963)
XLA Ops:
  0.6 1.2 copy.51
  1.8 0.5 copy.52
  2.3 26.5 %all_to_all.46 = f32[3,8,64,128]{3,1,0,2:T(8,128)} all-to-all(f32[3,8,64,128]{3,1,0,2:T(8,128)S(1)} %copy.52), channel_id=1, replica_groups=mesh['gx'=8,'gy'=4] {'gy'}, dimensions={2} | all-to-all | bytes 1572864 | tf_op jit(solution)/shard_map/all_to_all | solution.py:137
  28.8 3.7 %all-to-all-start.1 = ((f32[3,8,64,128]{3,1,0,2:T(8,128)}), f32[3,8,64,128]{3,1,0,2:T(8,128)S(1)}, u32[]{:S(2)}, u32[]{:S(2)}) async-start(f32[3,8,64,128]{3,1,0,2:T(8,128)} %all_to_all.46), calls=%async_computation.1 | async-start | bytes 1572864 | tf_op jit(solution)/shard_map/all_to_all | solution.py:136
  32.5 0.3 fusion.137
  32.9 12.2 %all-to-all-done.1 = f32[3,8,64,128]{3,1,0,2:T(8,128)S(1)} async-done(((f32[3,8,64,128]{3,1,0,2:T(8,128)}), f32[3,8,64,128]{3,1,0,2:T(8,128)S(1)}, u32[]{:S(2)}, u32[]{:S(2)}) %all-to-all-start.1) | async-done | bytes 786464 | tf_op jit(solution)/shard_map/all_to_all | solution.py:136
  45.2 2.1 %collective-permute-start = (f32[4,8,1,1024]{3,1,2,0:T(8,128)S(1)}, f32[4,8,1,1024]{3,1,2,0:T(8,128)S(1)}, u32[]{:S(2)}, u32[]{:S(2)}) collective-permute-start(f32[4,8,1,1024]{3,1,2,0:T(8,128)S(1)} %get-tuple-element.16), channel_id=1, source_target_pairs={{0,1},{1,2},{2,3},{3,4},{4,5},{5,6},{6,7},{7,8},{8,9},{9,10},{10,1... | collective-permute-start | bytes 393224 | tf_op jit(solution)/shard_map/ppermute | solution.py:20
  47.3 1.3 collective-permute-start.1
  48.6 1.2 collective-permute-done
  49.8 4.8 %collective-permute-done.1 = f32[4,8,1,1024]{3,1,2,0:T(8,128)S(1)} collective-permute-done((f32[4,8,1,1024]{3,1,2,0:T(8,128)S(1)}, f32[4,8,1,1024]{3,1,2,0:T(8,128)S(1)}, u32[]{:S(2)}, u32[]{:S(2)}) %collective-permute-start.1) | collective-permute-done | bytes 131104 | tf_op jit(solution)/shard_map/ppermute | solution.py:22
  54.7 0.4 select_maximum_fusion
  55.2 0.5 fusion.29
  55.7 0.6 copy-done
  56.4 1.4 broadcast_multiply_fusion
  57.8 2.5 %collective-permute-start.2 = (f32[1,8,1,1024]{3,1,2,0:T(8,128)S(1)}, f32[1,8,1,1024]{3,1,2,0:T(8,128)S(1)}, u32[]{:S(2)}, u32[]{:S(2)}) collective-permute-start(f32[1,8,1,1024]{3,1,2,0:T(8,128)S(1)} %get-tuple-element.20), channel_id=1, source_target_pairs={{0,1},{1,2},{2,3},{3,4},{4,5},{5,6},{6,7},{7,8},{8,9},{9,10},{10,1... | collective-permute-start | bytes 98312 | tf_op jit(solution)/shard_map/ppermute | solution.py:20
  60.3 1.3 collective-permute-start.3
  61.9 4.7 %collective-permute-done.3 = f32[1,8,1,1024]{3,1,2,0:T(8,128)S(1)} collective-permute-done((f32[1,8,1,1024]{3,1,2,0:T(8,128)S(1)}, f32[1,8,1,1024]{3,1,2,0:T(8,128)S(1)}, u32[]{:S(2)}, u32[]{:S(2)}) %collective-permute-start.3) | collective-permute-done | bytes 32800 | tf_op jit(solution)/shard_map/ppermute | solution.py:22
  66.8 0.4 fusion.124
  67.2 3.9 %collective-permute-start.4 = (f32[8,1,1024]{2,0,1:T(8,128)S(1)}, f32[8,1,1024]{2,0,1:T(8,128)S(1)}, u32[]{:S(2)}, u32[]{:S(2)}) collective-permute-start(f32[8,1,1024]{2,0,1:T(8,128)S(1)} %get-tuple-element.46), channel_id=1, source_target_pairs={{0,1},{1,2},{2,3},{3,4},{4,5},{5,6},{6,7},{7,8},{8,9},{9,10},{10,1... | collective-permute-start | bytes 98312 | tf_op jit(solution)/shard_map/ppermute | solution.py:20
  71.2 1.3 collective-permute-start.5
  72.5 0.3 collective-permute-done.4
  72.7 4.2 %collective-permute-done.5 = f32[8,1,1024]{2,0,1:T(8,128)S(1)} collective-permute-done((f32[8,1,1024]{2,0,1:T(8,128)S(1)}, f32[8,1,1024]{2,0,1:T(8,128)S(1)}, u32[]{:S(2)}, u32[]{:S(2)}) %collective-permute-start.5) | collective-permute-done | bytes 32800 | tf_op jit(solution)/shard_map/ppermute | solution.py:22
  77.1 0.4 fusion.39
  77.6 2.2 %collective-permute-start.6 = (f32[8,1,1024]{2,0,1:T(8,128)S(1)}, f32[8,1,1024]{2,0,1:T(8,128)S(1)}, u32[]{:S(2)}, u32[]{:S(2)}) collective-permute-start(f32[8,1,1024]{2,0,1:T(8,128)S(1)} %get-tuple-element.44), channel_id=1, source_target_pairs={{0,1},{1,2},{2,3},{3,4},{4,5},{5,6},{6,7},{7,8},{8,9},{9,10},{10,1... | collective-permute-start | bytes 98312 | tf_op jit(solution)/shard_map/ppermute | solution.py:20
  79.8 1.3 collective-permute-start.7
  81.1 0.3 collective-permute-done.6
  81.4 4.2 %collective-permute-done.7 = f32[8,1,1024]{2,0,1:T(8,128)S(1)} collective-permute-done((f32[8,1,1024]{2,0,1:T(8,128)S(1)}, f32[8,1,1024]{2,0,1:T(8,128)S(1)}, u32[]{:S(2)}, u32[]{:S(2)}) %collective-permute-start.7) | collective-permute-done | bytes 32800 | tf_op jit(solution)/shard_map/ppermute | solution.py:22
  85.8 0.4 fusion.48
  86.3 2.9 %collective-permute-start.8 = (f32[8,1,1024]{2,0,1:T(8,128)S(1)}, f32[8,1,1024]{2,0,1:T(8,128)S(1)}, u32[]{:S(2)}, u32[]{:S(2)}) collective-permute-start(f32[8,1,1024]{2,0,1:T(8,128)S(1)} %get-tuple-element.42), channel_id=1, source_target_pairs={{0,1},{1,2},{2,3},{3,4},{4,5},{5,6},{6,7},{7,8},{8,9},{9,10},{10,1... | collective-permute-start | bytes 98312 | tf_op jit(solution)/shard_map/ppermute | solution.py:20
  89.2 1.3 collective-permute-start.9
  90.8 4.2 %collective-permute-done.9 = f32[8,1,1024]{2,0,1:T(8,128)S(1)} collective-permute-done((f32[8,1,1024]{2,0,1:T(8,128)S(1)}, f32[8,1,1024]{2,0,1:T(8,128)S(1)}, u32[]{:S(2)}, u32[]{:S(2)}) %collective-permute-start.9) | collective-permute-done | bytes 32800 | tf_op jit(solution)/shard_map/ppermute | solution.py:22
  95.2 0.4 fusion.57
  95.6 4.1 %collective-permute-start.10 = (f32[8,1,1024]{2,0,1:T(8,128)S(1)}, f32[8,1,1024]{2,0,1:T(8,128)S(1)}, u32[]{:S(2)}, u32[]{:S(2)}) collective-permute-start(f32[8,1,1024]{2,0,1:T(8,128)S(1)} %get-tuple-element.40), channel_id=1, source_target_pairs={{0,1},{1,2},{2,3},{3,4},{4,5},{5,6},{6,7},{7,8},{8,9},{9,10},{10,1... | collective-permute-start | bytes 98312 | tf_op jit(solution)/shard_map/ppermute | solution.py:20
  99.7 1.3 collective-permute-start.11
  101.3 4.6 %collective-permute-done.11 = f32[8,1,1024]{2,0,1:T(8,128)S(1)} collective-permute-done((f32[8,1,1024]{2,0,1:T(8,128)S(1)}, f32[8,1,1024]{2,0,1:T(8,128)S(1)}, u32[]{:S(2)}, u32[]{:S(2)}) %collective-permute-start.11) | collective-permute-done | bytes 32800 | tf_op jit(solution)/shard_map/ppermute | solution.py:22
  106.1 0.4 fusion.66
  106.5 3.9 %collective-permute-start.12 = (f32[8,1,1024]{2,0,1:T(8,128)S(1)}, f32[8,1,1024]{2,0,1:T(8,128)S(1)}, u32[]{:S(2)}, u32[]{:S(2)}) collective-permute-start(f32[8,1,1024]{2,0,1:T(8,128)S(1)} %get-tuple-element.38), channel_id=1, source_target_pairs={{0,1},{1,2},{2,3},{3,4},{4,5},{5,6},{6,7},{7,8},{8,9},{9,10},{10,1... | collective-permute-start | bytes 98312 | tf_op jit(solution)/shard_map/ppermute | solution.py:20
  110.5 1.3 collective-permute-start.13
  112.1 4.6 %collective-permute-done.13 = f32[8,1,1024]{2,0,1:T(8,128)S(1)} collective-permute-done((f32[8,1,1024]{2,0,1:T(8,128)S(1)}, f32[8,1,1024]{2,0,1:T(8,128)S(1)}, u32[]{:S(2)}, u32[]{:S(2)}) %collective-permute-start.13) | collective-permute-done | bytes 32800 | tf_op jit(solution)/shard_map/ppermute | solution.py:22
  116.8 0.4 fusion.75
  117.3 3.7 %collective-permute-start.14 = (f32[8,1,1024]{2,0,1:T(8,128)S(1)}, f32[8,1,1024]{2,0,1:T(8,128)S(1)}, u32[]{:S(2)}, u32[]{:S(2)}) collective-permute-start(f32[8,1,1024]{2,0,1:T(8,128)S(1)} %get-tuple-element.36), channel_id=1, source_target_pairs={{0,1},{1,2},{2,3},{3,4},{4,5},{5,6},{6,7},{7,8},{8,9},{9,10},{10,1... | collective-permute-start | bytes 98312 | tf_op jit(solution)/shard_map/ppermute | solution.py:20
  121.0 1.3 collective-permute-start.15
  122.6 4.6 %collective-permute-done.15 = f32[8,1,1024]{2,0,1:T(8,128)S(1)} collective-permute-done((f32[8,1,1024]{2,0,1:T(8,128)S(1)}, f32[8,1,1024]{2,0,1:T(8,128)S(1)}, u32[]{:S(2)}, u32[]{:S(2)}) %collective-permute-start.15) | collective-permute-done | bytes 32800 | tf_op jit(solution)/shard_map/ppermute | solution.py:22
  127.3 0.4 fusion.84
  127.7 3.7 %collective-permute-start.16 = (f32[8,1,1024]{2,0,1:T(8,128)S(1)}, f32[8,1,1024]{2,0,1:T(8,128)S(1)}, u32[]{:S(2)}, u32[]{:S(2)}) collective-permute-start(f32[8,1,1024]{2,0,1:T(8,128)S(1)} %get-tuple-element.34), channel_id=1, source_target_pairs={{0,1},{1,2},{2,3},{3,4},{4,5},{5,6},{6,7},{7,8},{8,9},{9,10},{10,1... | collective-permute-start | bytes 98312 | tf_op jit(solution)/shard_map/ppermute | solution.py:20
  131.5 1.3 collective-permute-start.17
  132.8 0.3 collective-permute-done.16
  133.0 4.6 %collective-permute-done.17 = f32[8,1,1024]{2,0,1:T(8,128)S(1)} collective-permute-done((f32[8,1,1024]{2,0,1:T(8,128)S(1)}, f32[8,1,1024]{2,0,1:T(8,128)S(1)}, u32[]{:S(2)}, u32[]{:S(2)}) %collective-permute-start.17) | collective-permute-done | bytes 32800 | tf_op jit(solution)/shard_map/ppermute | solution.py:22
  137.8 0.4 fusion.93
  138.2 1.3 collective-permute-start.18
  139.5 4.5 %collective-permute-start.19 = (f32[8,1,1024]{2,0,1:T(8,128)S(1)}, f32[8,1,1024]{2,0,1:T(8,128)S(1)}, u32[]{:S(2)}, u32[]{:S(2)}) collective-permute-start(f32[8,1,1024]{2,0,1:T(8,128)S(1)} %get-tuple-element.32), channel_id=1, source_target_pairs={{0,1},{1,2},{2,3},{3,4},{4,5},{5,6},{6,7},{7,8},{8,9},{9,10},{10,1... | collective-permute-start | bytes 98312 | tf_op jit(solution)/shard_map/ppermute | solution.py:20
  144.1 2.7 %copy.58 = f32[1,8,8,1024]{2,1,0,3:T(8,128)} copy(f32[1,8,8,1024]{3,1,2,0:T(8,128)S(1)} %bitcast.42) | data formatting | bytes 524288 | tf_op jit(solution)/shard_map/broadcast_in_dim | solution.py:164
  146.8 4.4 %reshape.29 = f32[8,1,8192]{2,1,0:T(1,128)} reshape(f32[1024,1,8,8]{3,2,1,0:T(8,128)} %bitcast.38) | data formatting | bytes 524288
  151.2 18.5 %all-to-all-start.2 = ((f32[8,1,8192]{2,1,0:T(1,128)}), f32[8,1,8192]{2,1,0:T(1,128)S(1)}, u32[]{:S(2)}, u32[]{:S(2)}) async-start(f32[8,1,8192]{2,1,0:T(1,128)} %reshape.29), calls=%async_computation.2 | async-start | bytes 524288 | tf_op jit(solution)/shard_map/all_to_all | solution.py:125
  169.8 6.7 %all-to-all-done.2 = f32[8,1,8192]{2,1,0:T(1,128)S(1)} async-done(((f32[8,1,8192]{2,1,0:T(1,128)}), f32[8,1,8192]{2,1,0:T(1,128)S(1)}, u32[]{:S(2)}, u32[]{:S(2)}) %all-to-all-start.2) | async-done | bytes 262176 | tf_op jit(solution)/shard_map/all_to_all | solution.py:125
  176.5 0.5 broadcast.218
  177.1 1.3 reduce
  178.4 4.3 %reshape.30 = f32[1024,1,8,8]{3,2,1,0:T(8,128)} reshape(f32[8,8192]{1,0:T(8,128)S(1)} %reduce) | data formatting | bytes 524288
  182.7 3.5 %copy.59 = f32[1,8,8,8,128]{4,1,3,2,0:T(8,128)} copy(f32[1,8,8,8,128]{3,1,4,2,0:T(8,128)} %bitcast.37) | data formatting | bytes 524288 | tf_op jit(solution)/shard_map/all_to_all | solution.py:125
  186.1 5.7 %all-to-all-start.3 = ((f32[1,8,64,128]{3,1,0,2:T(8,128)}), f32[1,8,64,128]{3,1,0,2:T(8,128)S(1)}, u32[]{:S(2)}, u32[]{:S(2)}) async-start(f32[1,8,64,128]{3,1,0,2:T(8,128)} %bitcast.14), calls=%async_computation.3 | async-start | bytes 524288 | tf_op jit(solution)/shard_map/all_to_all | solution.py:124
  192.2 1.3 copy.62
  193.6 1.3 copy.63
  194.9 5.2 %all-to-all-done.3 = f32[1,8,64,128]{3,1,0,2:T(8,128)S(1)} async-done(((f32[1,8,64,128]{3,1,0,2:T(8,128)}), f32[1,8,64,128]{3,1,0,2:T(8,128)S(1)}, u32[]{:S(2)}, u32[]{:S(2)}) %all-to-all-start.3) | async-done | bytes 262176 | tf_op jit(solution)/shard_map/all_to_all | solution.py:124
  200.2 0.7 copy.61
  (40 shorter events, 3.6 us)
Async XLA Ops:
  2.3 30.2 %copy-start.1 = (f32[8,8,1024]{2,1,0:T(8,128)S(1)}, f32[8,8,1024]{2,1,0:T(8,128)}, u32[]{:S(2)}) copy-start(f32[8,8,1024]{2,1,0:T(8,128)} %param.5) | copy-start | bytes 786436
  2.3 30.2 %copy-start.2 = (s32[8,8,1024]{2,1,0:T(8,128)S(1)}, s32[8,8,1024]{2,1,0:T(8,128)}, u32[]{:S(2)}) copy-start(s32[8,8,1024]{2,1,0:T(8,128)} %param.4) | copy-start | bytes 786436
  28.8 16.3 %all-to-all-start.1 = ((f32[3,8,64,128]{3,1,0,2:T(8,128)}), f32[3,8,64,128]{3,1,0,2:T(8,128)S(1)}, u32[]{:S(2)}, u32[]{:S(2)}) async-start(f32[3,8,64,128]{3,1,0,2:T(8,128)} %all_to_all.46), calls=%async_computation.1 | async-start | bytes 1572864 | tf_op jit(solution)/shard_map/all_to_all | solution.py:136
  45.2 4.6 %collective-permute-start = (f32[4,8,1,1024]{3,1,2,0:T(8,128)S(1)}, f32[4,8,1,1024]{3,1,2,0:T(8,128)S(1)}, u32[]{:S(2)}, u32[]{:S(2)}) collective-permute-start(f32[4,8,1,1024]{3,1,2,0:T(8,128)S(1)} %get-tuple-element.16), channel_id=1, source_target_pairs={{0,1},{1,2},{2,3},{3,4},{4,5},{5,6},{6,7},{7,8},{8,9},{9,10},{10,1... | collective-permute-start | bytes 393224 | tf_op jit(solution)/shard_map/ppermute | solution.py:20
  47.3 7.3 %collective-permute-start.1 = (f32[4,8,1,1024]{3,1,2,0:T(8,128)S(1)}, f32[4,8,1,1024]{3,1,2,0:T(8,128)S(1)}, u32[]{:S(2)}, u32[]{:S(2)}) collective-permute-start(f32[4,8,1,1024]{3,1,2,0:T(8,128)S(1)} %get-tuple-element.17), channel_id=1, source_target_pairs={{1,0},{2,1},{3,2},{4,3},{5,4},{6,5},{7,6},{8,7},{9,8},{10,9},{11,1... | collective-permute-start | bytes 393224 | tf_op jit(solution)/shard_map/ppermute | solution.py:22
  55.2 1.1 copy-start
  57.8 4.1 %collective-permute-start.2 = (f32[1,8,1,1024]{3,1,2,0:T(8,128)S(1)}, f32[1,8,1,1024]{3,1,2,0:T(8,128)S(1)}, u32[]{:S(2)}, u32[]{:S(2)}) collective-permute-start(f32[1,8,1,1024]{3,1,2,0:T(8,128)S(1)} %get-tuple-element.20), channel_id=1, source_target_pairs={{0,1},{1,2},{2,3},{3,4},{4,5},{5,6},{6,7},{7,8},{8,9},{9,10},{10,1... | collective-permute-start | bytes 98312 | tf_op jit(solution)/shard_map/ppermute | solution.py:20
  60.3 6.3 %collective-permute-start.3 = (f32[1,8,1,1024]{3,1,2,0:T(8,128)S(1)}, f32[1,8,1,1024]{3,1,2,0:T(8,128)S(1)}, u32[]{:S(2)}, u32[]{:S(2)}) collective-permute-start(f32[1,8,1,1024]{3,1,2,0:T(8,128)S(1)} %get-tuple-element.21), channel_id=1, source_target_pairs={{1,0},{2,1},{3,2},{4,3},{5,4},{6,5},{7,6},{8,7},{9,8},{10,9},{11,1... | collective-permute-start | bytes 98312 | tf_op jit(solution)/shard_map/ppermute | solution.py:22
  67.2 5.5 %collective-permute-start.4 = (f32[8,1,1024]{2,0,1:T(8,128)S(1)}, f32[8,1,1024]{2,0,1:T(8,128)S(1)}, u32[]{:S(2)}, u32[]{:S(2)}) collective-permute-start(f32[8,1,1024]{2,0,1:T(8,128)S(1)} %get-tuple-element.46), channel_id=1, source_target_pairs={{0,1},{1,2},{2,3},{3,4},{4,5},{5,6},{6,7},{7,8},{8,9},{9,10},{10,1... | collective-permute-start | bytes 98312 | tf_op jit(solution)/shard_map/ppermute | solution.py:20
  71.2 5.8 %collective-permute-start.5 = (f32[8,1,1024]{2,0,1:T(8,128)S(1)}, f32[8,1,1024]{2,0,1:T(8,128)S(1)}, u32[]{:S(2)}, u32[]{:S(2)}) collective-permute-start(f32[8,1,1024]{2,0,1:T(8,128)S(1)} %get-tuple-element.47), channel_id=1, source_target_pairs={{1,0},{2,1},{3,2},{4,3},{5,4},{6,5},{7,6},{8,7},{9,8},{10,9},{11,1... | collective-permute-start | bytes 98312 | tf_op jit(solution)/shard_map/ppermute | solution.py:22
  77.6 3.8 %collective-permute-start.6 = (f32[8,1,1024]{2,0,1:T(8,128)S(1)}, f32[8,1,1024]{2,0,1:T(8,128)S(1)}, u32[]{:S(2)}, u32[]{:S(2)}) collective-permute-start(f32[8,1,1024]{2,0,1:T(8,128)S(1)} %get-tuple-element.44), channel_id=1, source_target_pairs={{0,1},{1,2},{2,3},{3,4},{4,5},{5,6},{6,7},{7,8},{8,9},{9,10},{10,1... | collective-permute-start | bytes 98312 | tf_op jit(solution)/shard_map/ppermute | solution.py:20
  79.8 5.8 %collective-permute-start.7 = (f32[8,1,1024]{2,0,1:T(8,128)S(1)}, f32[8,1,1024]{2,0,1:T(8,128)S(1)}, u32[]{:S(2)}, u32[]{:S(2)}) collective-permute-start(f32[8,1,1024]{2,0,1:T(8,128)S(1)} %get-tuple-element.45), channel_id=1, source_target_pairs={{1,0},{2,1},{3,2},{4,3},{5,4},{6,5},{7,6},{8,7},{9,8},{10,9},{11,1... | collective-permute-start | bytes 98312 | tf_op jit(solution)/shard_map/ppermute | solution.py:22
  86.3 4.5 %collective-permute-start.8 = (f32[8,1,1024]{2,0,1:T(8,128)S(1)}, f32[8,1,1024]{2,0,1:T(8,128)S(1)}, u32[]{:S(2)}, u32[]{:S(2)}) collective-permute-start(f32[8,1,1024]{2,0,1:T(8,128)S(1)} %get-tuple-element.42), channel_id=1, source_target_pairs={{0,1},{1,2},{2,3},{3,4},{4,5},{5,6},{6,7},{7,8},{8,9},{9,10},{10,1... | collective-permute-start | bytes 98312 | tf_op jit(solution)/shard_map/ppermute | solution.py:20
  89.2 5.8 %collective-permute-start.9 = (f32[8,1,1024]{2,0,1:T(8,128)S(1)}, f32[8,1,1024]{2,0,1:T(8,128)S(1)}, u32[]{:S(2)}, u32[]{:S(2)}) collective-permute-start(f32[8,1,1024]{2,0,1:T(8,128)S(1)} %get-tuple-element.43), channel_id=1, source_target_pairs={{1,0},{2,1},{3,2},{4,3},{5,4},{6,5},{7,6},{8,7},{9,8},{10,9},{11,1... | collective-permute-start | bytes 98312 | tf_op jit(solution)/shard_map/ppermute | solution.py:22
  95.6 5.7 %collective-permute-start.10 = (f32[8,1,1024]{2,0,1:T(8,128)S(1)}, f32[8,1,1024]{2,0,1:T(8,128)S(1)}, u32[]{:S(2)}, u32[]{:S(2)}) collective-permute-start(f32[8,1,1024]{2,0,1:T(8,128)S(1)} %get-tuple-element.40), channel_id=1, source_target_pairs={{0,1},{1,2},{2,3},{3,4},{4,5},{5,6},{6,7},{7,8},{8,9},{9,10},{10,1... | collective-permute-start | bytes 98312 | tf_op jit(solution)/shard_map/ppermute | solution.py:20
  99.7 6.2 %collective-permute-start.11 = (f32[8,1,1024]{2,0,1:T(8,128)S(1)}, f32[8,1,1024]{2,0,1:T(8,128)S(1)}, u32[]{:S(2)}, u32[]{:S(2)}) collective-permute-start(f32[8,1,1024]{2,0,1:T(8,128)S(1)} %get-tuple-element.41), channel_id=1, source_target_pairs={{1,0},{2,1},{3,2},{4,3},{5,4},{6,5},{7,6},{8,7},{9,8},{10,9},{11,1... | collective-permute-start | bytes 98312 | tf_op jit(solution)/shard_map/ppermute | solution.py:22
  106.5 5.5 %collective-permute-start.12 = (f32[8,1,1024]{2,0,1:T(8,128)S(1)}, f32[8,1,1024]{2,0,1:T(8,128)S(1)}, u32[]{:S(2)}, u32[]{:S(2)}) collective-permute-start(f32[8,1,1024]{2,0,1:T(8,128)S(1)} %get-tuple-element.38), channel_id=1, source_target_pairs={{0,1},{1,2},{2,3},{3,4},{4,5},{5,6},{6,7},{7,8},{8,9},{9,10},{10,1... | collective-permute-start | bytes 98312 | tf_op jit(solution)/shard_map/ppermute | solution.py:20
  110.5 6.1 %collective-permute-start.13 = (f32[8,1,1024]{2,0,1:T(8,128)S(1)}, f32[8,1,1024]{2,0,1:T(8,128)S(1)}, u32[]{:S(2)}, u32[]{:S(2)}) collective-permute-start(f32[8,1,1024]{2,0,1:T(8,128)S(1)} %get-tuple-element.39), channel_id=1, source_target_pairs={{1,0},{2,1},{3,2},{4,3},{5,4},{6,5},{7,6},{8,7},{9,8},{10,9},{11,1... | collective-permute-start | bytes 98312 | tf_op jit(solution)/shard_map/ppermute | solution.py:22
  117.3 5.3 %collective-permute-start.14 = (f32[8,1,1024]{2,0,1:T(8,128)S(1)}, f32[8,1,1024]{2,0,1:T(8,128)S(1)}, u32[]{:S(2)}, u32[]{:S(2)}) collective-permute-start(f32[8,1,1024]{2,0,1:T(8,128)S(1)} %get-tuple-element.36), channel_id=1, source_target_pairs={{0,1},{1,2},{2,3},{3,4},{4,5},{5,6},{6,7},{7,8},{8,9},{9,10},{10,1... | collective-permute-start | bytes 98312 | tf_op jit(solution)/shard_map/ppermute | solution.py:20
  121.0 6.1 %collective-permute-start.15 = (f32[8,1,1024]{2,0,1:T(8,128)S(1)}, f32[8,1,1024]{2,0,1:T(8,128)S(1)}, u32[]{:S(2)}, u32[]{:S(2)}) collective-permute-start(f32[8,1,1024]{2,0,1:T(8,128)S(1)} %get-tuple-element.37), channel_id=1, source_target_pairs={{1,0},{2,1},{3,2},{4,3},{5,4},{6,5},{7,6},{8,7},{9,8},{10,9},{11,1... | collective-permute-start | bytes 98312 | tf_op jit(solution)/shard_map/ppermute | solution.py:22
  127.7 5.3 %collective-permute-start.16 = (f32[8,1,1024]{2,0,1:T(8,128)S(1)}, f32[8,1,1024]{2,0,1:T(8,128)S(1)}, u32[]{:S(2)}, u32[]{:S(2)}) collective-permute-start(f32[8,1,1024]{2,0,1:T(8,128)S(1)} %get-tuple-element.34), channel_id=1, source_target_pairs={{0,1},{1,2},{2,3},{3,4},{4,5},{5,6},{6,7},{7,8},{8,9},{9,10},{10,1... | collective-permute-start | bytes 98312 | tf_op jit(solution)/shard_map/ppermute | solution.py:20
  131.5 6.1 %collective-permute-start.17 = (f32[8,1,1024]{2,0,1:T(8,128)S(1)}, f32[8,1,1024]{2,0,1:T(8,128)S(1)}, u32[]{:S(2)}, u32[]{:S(2)}) collective-permute-start(f32[8,1,1024]{2,0,1:T(8,128)S(1)} %get-tuple-element.35), channel_id=1, source_target_pairs={{1,0},{2,1},{3,2},{4,3},{5,4},{6,5},{7,6},{8,7},{9,8},{10,9},{11,1... | collective-permute-start | bytes 98312 | tf_op jit(solution)/shard_map/ppermute | solution.py:22
  138.2 31.4 %collective-permute-start.18 = (f32[8,1,1024]{2,0,1:T(8,128)S(1)}, f32[8,1,1024]{2,0,1:T(8,128)S(1)}, u32[]{:S(2)}, u32[]{:S(2)}) collective-permute-start(f32[8,1,1024]{2,0,1:T(8,128)S(1)} %get-tuple-element.33), channel_id=1, source_target_pairs={{1,0},{2,1},{3,2},{4,3},{5,4},{6,5},{7,6},{8,7},{9,8},{10,9},{11,1... | collective-permute-start | bytes 98312 | tf_op jit(solution)/shard_map/ppermute | solution.py:22
  139.5 30.1 %collective-permute-start.19 = (f32[8,1,1024]{2,0,1:T(8,128)S(1)}, f32[8,1,1024]{2,0,1:T(8,128)S(1)}, u32[]{:S(2)}, u32[]{:S(2)}) collective-permute-start(f32[8,1,1024]{2,0,1:T(8,128)S(1)} %get-tuple-element.32), channel_id=1, source_target_pairs={{0,1},{1,2},{2,3},{3,4},{4,5},{5,6},{6,7},{7,8},{8,9},{9,10},{10,1... | collective-permute-start | bytes 98312 | tf_op jit(solution)/shard_map/ppermute | solution.py:20
  151.2 25.4 %all-to-all-start.2 = ((f32[8,1,8192]{2,1,0:T(1,128)}), f32[8,1,8192]{2,1,0:T(1,128)S(1)}, u32[]{:S(2)}, u32[]{:S(2)}) async-start(f32[8,1,8192]{2,1,0:T(1,128)} %reshape.29), calls=%async_computation.2 | async-start | bytes 524288 | tf_op jit(solution)/shard_map/all_to_all | solution.py:125
  186.1 14.0 %all-to-all-start.3 = ((f32[1,8,64,128]{3,1,0,2:T(8,128)}), f32[1,8,64,128]{3,1,0,2:T(8,128)S(1)}, u32[]{:S(2)}, u32[]{:S(2)}) async-start(f32[1,8,64,128]{3,1,0,2:T(8,128)} %bitcast.14), calls=%async_computation.3 | async-start | bytes 524288 | tf_op jit(solution)/shard_map/all_to_all | solution.py:124
where the time goes:
time: 202 us; the launch traced here: 201 us
  starting transfers between devices  74.5 us (37%)
  waiting for transfers between devices  67.8 us (34%)
  blocking collectives  26.5 us (13%)
  local copies, waits for them, and re-layouts  21.6 us (11%)
  other arithmetic  9.39 us (5%)
    ppermute x10, waiting for transfers between devices, padded_2(): lax.ppermute(head, axis, [((i + 1) % count, i) for i in range(ends)])  40.5 us
    ppermute x10, starting transfers between devices, padded_2(): lax.ppermute(tail, axis, [(i, (i + 1) % count) for i in range(ends)])  33.7 us
    all_to_all x1, blocking collectives, to_particles(): lax.all_to_all(ordered, 'gy', split_axis=2, concat_axis=2, tiled=True)  26.5 us
    all_to_all x1, starting transfers between devices, to_fluid(): lax.all_to_all(fields, 'gx', split_axis=3, concat_axis=2, tiled=True)  18.5 us
    ppermute x10, starting transfers between devices, padded_2(): lax.ppermute(head, axis, [((i + 1) % count, i) for i in range(ends)])  12.9 us
    all_to_all x1, waiting for transfers between devices, to_particles(): lax.all_to_all(lax.all_to_all(ordered, 'gy', split_axis=2, concat_axis=2,...  12.2 us
    unnamed x10, local copies, waits for them, and re-layouts  12.1 us
    all_to_all x1, waiting for transfers between devices, to_fluid(): lax.all_to_all(fields, 'gx', split_axis=3, concat_axis=2, tiled=True)  6.72 us
  transfers between devices with their start and end apart: 23, of which 20 were waited for; matrix products, arithmetic and copies ran while one was open for 5% of the time, Pallas kernels for 0%

commit v1 on v0

--- a/solution.py
+++ b/solution.py
@@ -122,7 +122,10 @@
 
 def to_fluid(fields):
     moved = lax.all_to_all(
-        lax.all_to_all(fields, "gx", split_axis=3, concat_axis=2, tiled=True),
+        jnp.concatenate(
+            lax.all_to_all(jnp.stack(jnp.split(fields, lax.axis_size("gx"), axis=3)), "gx", 0, 0),
+            axis=2,
+        ),
         "gy",
         split_axis=2,
         concat_axis=2,

time: 202 us -> 192 us (0.950)
  local copies, waits for them, and re-layouts: 21.6 us -> 10.1 us
  other arithmetic: 9.39 us -> 12.1 us
    unnamed x10 -> x13, local copies, waits for them, and re-layouts: 12.1 us -> 5.01 us
    all_to_all x3 -> x2, local copies, waits for them, and re-layouts: 4.02 us -> 0.07 us  [the longest x1 0.05 us: to_fluid(): lax.all_to_all(jnp.concatenate(lax.all_to_all(jnp.stack(jnp.split(fields,...]
    concatenate x9, other arithmetic: 1.73 us -> 4.76 us  [padded_2(): jnp.concatenate([lax.ppermute(tail, axis, [(i, (i + 1) % count) for i in...]
    broadcast_in_dim x1 -> x0, local copies, waits for them, and re-layouts: 2.66 us -> none  [shards(): pressure_out = to_fluid(pressure[None])[0]]
  transfers between devices with their start and end apart: 23 -> 23, of which waited for: 20 -> 20; matrix products, arithmetic and copies ran while one was open for 5% -> 4% of each run, Pallas kernels for 0% -> 0%
where the time goes in v1:
time: 192 us; the launch traced here: 191 us
  starting transfers between devices  72.6 us (38%)
  waiting for transfers between devices  69.2 us (36%)
  blocking collectives  26.4 us (14%)
  other arithmetic  12.1 us (6%)
  local copies, waits for them, and re-layouts  10.1 us (5%)
    ppermute x10, waiting for transfers between devices, padded_2(): lax.ppermute(head, axis, [((i + 1) % count, i) for i in range(ends)])  40.3 us
    ppermute x10, starting transfers between devices, padded_2(): lax.ppermute(tail, axis, [(i, (i + 1) % count) for i in range(ends)])  32.8 us
    all_to_all x1, blocking collectives, to_particles(): lax.all_to_all(ordered, 'gy', split_axis=2, concat_axis=2, tiled=True)  26.4 us
    all_to_all x1, starting transfers between devices, to_fluid(): lax.all_to_all(jnp.stack(jnp.split(fields, lax.axis_size('gx'), axis=3)),...  19.5 us
    ppermute x10, starting transfers between devices, padded_2(): lax.ppermute(head, axis, [((i + 1) % count, i) for i in range(ends)])  13.1 us
    all_to_all x1, waiting for transfers between devices, to_particles(): lax.all_to_all(lax.all_to_all(ordered, 'gy', split_axis=2, concat_axis=2,...  12.5 us
    all_to_all x1, waiting for transfers between devices, to_fluid(): lax.all_to_all(jnp.concatenate(lax.all_to_all(jnp.stack(jnp.split(fields,...  6.95 us
    all_to_all x1, waiting for transfers between devices, to_fluid(): lax.all_to_all(jnp.stack(jnp.split(fields, lax.axis_size('gx'), axis=3)),...  6.47 us
  transfers between devices with their start and end apart: 23, of which 20 were waited for; matrix products, arithmetic and copies ran while one was open for 4% of the time, Pallas kernels for 0%

profile of v1, /device:TPU:0, one launch (start us, length us, event | category | flops | bytes accessed | tf_op | source)
XLA Modules:
  0.0 191.4 jit_solution(9085859383611775097)
XLA Ops:
  0.6 1.2 copy.23
  1.9 0.5 copy.24
  2.3 26.4 %all_to_all.33 = f32[3,8,64,128]{3,1,0,2:T(8,128)} all-to-all(f32[3,8,64,128]{3,1,0,2:T(8,128)S(1)} %copy.24), channel_id=1, replica_groups=mesh['gx'=8,'gy'=4] {'gy'}, dimensions={2} | all-to-all | bytes 1572864 | tf_op jit(solution)/shard_map/all_to_all | solution.py:140
  28.7 3.7 %all-to-all-start.1 = ((f32[3,8,64,128]{3,1,0,2:T(8,128)}), f32[3,8,64,128]{3,1,0,2:T(8,128)S(1)}, u32[]{:S(2)}, u32[]{:S(2)}) async-start(f32[3,8,64,128]{3,1,0,2:T(8,128)} %all_to_all.33), calls=%async_computation.1 | async-start | bytes 1572864 | tf_op jit(solution)/shard_map/all_to_all | solution.py:139
  32.5 12.5 %all-to-all-done.1 = f32[3,8,64,128]{3,1,0,2:T(8,128)S(1)} async-done(((f32[3,8,64,128]{3,1,0,2:T(8,128)}), f32[3,8,64,128]{3,1,0,2:T(8,128)S(1)}, u32[]{:S(2)}, u32[]{:S(2)}) %all-to-all-start.1) | async-done | bytes 786464 | tf_op jit(solution)/shard_map/all_to_all | solution.py:139
  45.3 2.1 %collective-permute-start = (f32[4,8,1,1024]{3,2,1,0:T(1,128)S(1)}, f32[4,8,1,1024]{3,2,1,0:T(1,128)S(1)}, u32[]{:S(2)}, u32[]{:S(2)}) collective-permute-start(f32[4,8,1,1024]{3,2,1,0:T(1,128)S(1)} %get-tuple-element.9), channel_id=1, source_target_pairs={{0,1},{1,2},{2,3},{3,4},{4,5},{5,6},{6,7},{7,8},{8,9},{9,10},{10,1... | collective-permute-start | bytes 393224 | tf_op jit(solution)/shard_map/ppermute | solution.py:20
  47.4 1.3 collective-permute-start.1
  48.7 1.2 collective-permute-done
  49.9 4.8 %collective-permute-done.1 = f32[4,8,1,1024]{3,2,1,0:T(1,128)S(1)} collective-permute-done((f32[4,8,1,1024]{3,2,1,0:T(1,128)S(1)}, f32[4,8,1,1024]{3,2,1,0:T(1,128)S(1)}, u32[]{:S(2)}, u32[]{:S(2)}) %collective-permute-start.1) | collective-permute-done | bytes 131104 | tf_op jit(solution)/shard_map/ppermute | solution.py:22
  54.7 1.4 select_maximum_fusion
  56.4 0.5 fusion.28
  56.8 0.7 copy-done.1
  57.5 1.3 broadcast_multiply_fusion
  58.9 2.5 %collective-permute-start.2 = (f32[1,8,1,1024]{3,2,1,0:T(1,128)S(1)}, f32[1,8,1,1024]{3,2,1,0:T(1,128)S(1)}, u32[]{:S(2)}, u32[]{:S(2)}) collective-permute-start(f32[1,8,1,1024]{3,2,1,0:T(1,128)S(1)} %get-tuple-element.11), channel_id=1, source_target_pairs={{0,1},{1,2},{2,3},{3,4},{4,5},{5,6},{6,7},{7,8},{8,9},{9,10},{10,1... | collective-permute-start | bytes 98312 | tf_op jit(solution)/shard_map/ppermute | solution.py:20
  61.4 1.3 collective-permute-start.3
  62.6 0.4 fusion.20
  63.1 4.5 %collective-permute-done.3 = f32[1,8,1,1024]{3,2,1,0:T(1,128)S(1)} collective-permute-done((f32[1,8,1,1024]{3,2,1,0:T(1,128)S(1)}, f32[1,8,1,1024]{3,2,1,0:T(1,128)S(1)}, u32[]{:S(2)}, u32[]{:S(2)}) %collective-permute-start.3) | collective-permute-done | bytes 32800 | tf_op jit(solution)/shard_map/ppermute | solution.py:22
  67.6 0.4 fusion.22
  68.1 0.5 fusion.121
  68.6 3.9 %collective-permute-start.4 = (f32[8,1,1024]{2,1,0:T(1,128)S(1)}, f32[8,1,1024]{2,1,0:T(1,128)S(1)}, u32[]{:S(2)}, u32[]{:S(2)}) collective-permute-start(f32[8,1,1024]{2,1,0:T(1,128)S(1)} %get-tuple-element.37), channel_id=1, source_target_pairs={{0,1},{1,2},{2,3},{3,4},{4,5},{5,6},{6,7},{7,8},{8,9},{9,10},{10,1... | collective-permute-start | bytes 98312 | tf_op jit(solution)/shard_map/ppermute | solution.py:20
  72.5 1.3 collective-permute-start.5
  74.1 4.2 %collective-permute-done.5 = f32[8,1,1024]{2,1,0:T(1,128)S(1)} collective-permute-done((f32[8,1,1024]{2,1,0:T(1,128)S(1)}, f32[8,1,1024]{2,1,0:T(1,128)S(1)}, u32[]{:S(2)}, u32[]{:S(2)}) %collective-permute-start.5) | collective-permute-done | bytes 32800 | tf_op jit(solution)/shard_map/ppermute | solution.py:22
  78.3 0.4 select_maximum_fusion.17
  79.2 2.2 %collective-permute-start.6 = (f32[8,1,1024]{2,1,0:T(1,128)S(1)}, f32[8,1,1024]{2,1,0:T(1,128)S(1)}, u32[]{:S(2)}, u32[]{:S(2)}) collective-permute-start(f32[8,1,1024]{2,1,0:T(1,128)S(1)} %get-tuple-element.35), channel_id=1, source_target_pairs={{0,1},{1,2},{2,3},{3,4},{4,5},{5,6},{6,7},{7,8},{8,9},{9,10},{10,1... | collective-permute-start | bytes 98312 | tf_op jit(solution)/shard_map/ppermute | solution.py:20
  81.4 1.3 collective-permute-start.7
  83.0 4.2 %collective-permute-done.7 = f32[8,1,1024]{2,1,0:T(1,128)S(1)} collective-permute-done((f32[8,1,1024]{2,1,0:T(1,128)S(1)}, f32[8,1,1024]{2,1,0:T(1,128)S(1)}, u32[]{:S(2)}, u32[]{:S(2)}) %collective-permute-start.7) | collective-permute-done | bytes 32800 | tf_op jit(solution)/shard_map/ppermute | solution.py:22
  87.2 0.4 select_maximum_fusion.15
  88.1 2.9 %collective-permute-start.8 = (f32[8,1,1024]{2,1,0:T(1,128)S(1)}, f32[8,1,1024]{2,1,0:T(1,128)S(1)}, u32[]{:S(2)}, u32[]{:S(2)}) collective-permute-start(f32[8,1,1024]{2,1,0:T(1,128)S(1)} %get-tuple-element.33), channel_id=1, source_target_pairs={{0,1},{1,2},{2,3},{3,4},{4,5},{5,6},{6,7},{7,8},{8,9},{9,10},{10,1... | collective-permute-start | bytes 98312 | tf_op jit(solution)/shard_map/ppermute | solution.py:20
  91.0 1.3 collective-permute-start.9
  92.6 4.2 %collective-permute-done.9 = f32[8,1,1024]{2,1,0:T(1,128)S(1)} collective-permute-done((f32[8,1,1024]{2,1,0:T(1,128)S(1)}, f32[8,1,1024]{2,1,0:T(1,128)S(1)}, u32[]{:S(2)}, u32[]{:S(2)}) %collective-permute-start.9) | collective-permute-done | bytes 32800 | tf_op jit(solution)/shard_map/ppermute | solution.py:22
  96.9 0.4 select_maximum_fusion.13
  97.7 4.1 %collective-permute-start.10 = (f32[8,1,1024]{2,1,0:T(1,128)S(1)}, f32[8,1,1024]{2,1,0:T(1,128)S(1)}, u32[]{:S(2)}, u32[]{:S(2)}) collective-permute-start(f32[8,1,1024]{2,1,0:T(1,128)S(1)} %get-tuple-element.31), channel_id=1, source_target_pairs={{0,1},{1,2},{2,3},{3,4},{4,5},{5,6},{6,7},{7,8},{8,9},{9,10},{10,1... | collective-permute-start | bytes 98312 | tf_op jit(solution)/shard_map/ppermute | solution.py:20
  101.8 1.3 collective-permute-start.11
  103.4 4.6 %collective-permute-done.11 = f32[8,1,1024]{2,1,0:T(1,128)S(1)} collective-permute-done((f32[8,1,1024]{2,1,0:T(1,128)S(1)}, f32[8,1,1024]{2,1,0:T(1,128)S(1)}, u32[]{:S(2)}, u32[]{:S(2)}) %collective-permute-start.11) | collective-permute-done | bytes 32800 | tf_op jit(solution)/shard_map/ppermute | solution.py:22
  108.0 0.4 select_maximum_fusion.11
  108.9 3.9 %collective-permute-start.12 = (f32[8,1,1024]{2,1,0:T(1,128)S(1)}, f32[8,1,1024]{2,1,0:T(1,128)S(1)}, u32[]{:S(2)}, u32[]{:S(2)}) collective-permute-start(f32[8,1,1024]{2,1,0:T(1,128)S(1)} %get-tuple-element.29), channel_id=1, source_target_pairs={{0,1},{1,2},{2,3},{3,4},{4,5},{5,6},{6,7},{7,8},{8,9},{9,10},{10,1... | collective-permute-start | bytes 98312 | tf_op jit(solution)/shard_map/ppermute | solution.py:20
  112.8 1.3 collective-permute-start.13
  114.4 4.6 %collective-permute-done.13 = f32[8,1,1024]{2,1,0:T(1,128)S(1)} collective-permute-done((f32[8,1,1024]{2,1,0:T(1,128)S(1)}, f32[8,1,1024]{2,1,0:T(1,128)S(1)}, u32[]{:S(2)}, u32[]{:S(2)}) %collective-permute-start.13) | collective-permute-done | bytes 32800 | tf_op jit(solution)/shard_map/ppermute | solution.py:22
  119.0 0.4 select_maximum_fusion.9
  119.8 3.7 %collective-permute-start.14 = (f32[8,1,1024]{2,1,0:T(1,128)S(1)}, f32[8,1,1024]{2,1,0:T(1,128)S(1)}, u32[]{:S(2)}, u32[]{:S(2)}) collective-permute-start(f32[8,1,1024]{2,1,0:T(1,128)S(1)} %get-tuple-element.27), channel_id=1, source_target_pairs={{0,1},{1,2},{2,3},{3,4},{4,5},{5,6},{6,7},{7,8},{8,9},{9,10},{10,1... | collective-permute-start | bytes 98312 | tf_op jit(solution)/shard_map/ppermute | solution.py:20
  123.6 1.5 collective-permute-start.15
  125.1 4.6 %collective-permute-done.15 = f32[8,1,1024]{2,1,0:T(1,128)S(1)} collective-permute-done((f32[8,1,1024]{2,1,0:T(1,128)S(1)}, f32[8,1,1024]{2,1,0:T(1,128)S(1)}, u32[]{:S(2)}, u32[]{:S(2)}) %collective-permute-start.15) | collective-permute-done | bytes 32800 | tf_op jit(solution)/shard_map/ppermute | solution.py:22
  129.7 0.4 select_maximum_fusion.7
  130.6 3.7 %collective-permute-start.16 = (f32[8,1,1024]{2,1,0:T(1,128)S(1)}, f32[8,1,1024]{2,1,0:T(1,128)S(1)}, u32[]{:S(2)}, u32[]{:S(2)}) collective-permute-start(f32[8,1,1024]{2,1,0:T(1,128)S(1)} %get-tuple-element.25), channel_id=1, source_target_pairs={{0,1},{1,2},{2,3},{3,4},{4,5},{5,6},{6,7},{7,8},{8,9},{9,10},{10,1... | collective-permute-start | bytes 98312 | tf_op jit(solution)/shard_map/ppermute | solution.py:20
  134.3 1.3 collective-permute-start.17
  135.9 4.6 %collective-permute-done.17 = f32[8,1,1024]{2,1,0:T(1,128)S(1)} collective-permute-done((f32[8,1,1024]{2,1,0:T(1,128)S(1)}, f32[8,1,1024]{2,1,0:T(1,128)S(1)}, u32[]{:S(2)}, u32[]{:S(2)}) %collective-permute-start.17) | collective-permute-done | bytes 32800 | tf_op jit(solution)/shard_map/ppermute | solution.py:22
  140.4 0.4 select_maximum_fusion.5
  141.3 3.7 %collective-permute-start.19 = (f32[8,1,1024]{2,1,0:T(1,128)S(1)}, f32[8,1,1024]{2,1,0:T(1,128)S(1)}, u32[]{:S(2)}, u32[]{:S(2)}) collective-permute-start(f32[8,1,1024]{2,1,0:T(1,128)S(1)} %get-tuple-element.23), channel_id=1, source_target_pairs={{0,1},{1,2},{2,3},{3,4},{4,5},{5,6},{6,7},{7,8},{8,9},{9,10},{10,1... | collective-permute-start | bytes 98312 | tf_op jit(solution)/shard_map/ppermute | solution.py:20
  145.0 1.3 collective-permute-start.18
  146.3 0.6 fusion.129
  147.0 0.6 fusion.128
  147.6 0.6 fusion.127
  148.2 0.6 fusion.126
  148.8 0.6 fusion.125
  149.4 0.6 fusion.124
  150.1 0.6 fusion.123
  150.7 0.6 fusion.122
  151.3 19.5 %all-to-all-start.2 = ((f32[8,1,8,8,128]{4,3,2,1,0:T(8,128)}), f32[8,1,8,8,128]{4,3,2,1,0:T(8,128)S(1)}, u32[]{:S(2)}, u32[]{:S(2)}) async-start(f32[8,1,8,8,128]{4,3,2,1,0:T(8,128)} %fusion.122), calls=%async_computation.2 | async-start | bytes 524288 | tf_op jit(solution)/shard_map/all_to_all | solution.py:126
  171.2 6.5 %all-to-all-done.2 = f32[8,1,8,8,128]{4,3,2,1,0:T(8,128)S(1)} async-done(((f32[8,1,8,8,128]{4,3,2,1,0:T(8,128)}), f32[8,1,8,8,128]{4,3,2,1,0:T(8,128)S(1)}, u32[]{:S(2)}, u32[]{:S(2)}) %all-to-all-start.2) | async-done | bytes 262176 | tf_op jit(solution)/shard_map/all_to_all | solution.py:126
  177.7 0.9 copy.27
  178.6 3.4 %all-to-all-start.3 = ((f32[1,8,64,128]{3,1,0,2:T(8,128)}), f32[1,8,64,128]{3,1,0,2:T(8,128)S(1)}, u32[]{:S(2)}, u32[]{:S(2)}) async-start(f32[1,8,64,128]{3,1,0,2:T(8,128)} %copy.27), calls=%async_computation.3 | async-start | bytes 524288 | tf_op jit(solution)/shard_map/all_to_all | solution.py:124
  182.3 1.3 multiply_subtract_fusion
  183.6 7.0 %all-to-all-done.3 = f32[1,8,64,128]{3,1,0,2:T(8,128)S(1)} async-done(((f32[1,8,64,128]{3,1,0,2:T(8,128)}), f32[1,8,64,128]{3,1,0,2:T(8,128)S(1)}, u32[]{:S(2)}, u32[]{:S(2)}) %all-to-all-start.3) | async-done | bytes 262176 | tf_op jit(solution)/shard_map/all_to_all | solution.py:124
  190.6 0.7 copy.29
  (42 shorter events, 6.4 us)
Async XLA Ops:
  1.8 30.6 %copy-start = (f32[8,8,1024]{2,1,0:T(8,128)S(1)}, f32[8,8,1024]{2,1,0:T(8,128)}, u32[]{:S(2)}) copy-start(f32[8,8,1024]{2,1,0:T(8,128)} %param.5) | copy-start | bytes 786436
  1.8 30.6 %copy-start.2 = (s32[8,8,1024]{2,1,0:T(8,128)S(1)}, s32[8,8,1024]{2,1,0:T(8,128)}, u32[]{:S(2)}) copy-start(s32[8,8,1024]{2,1,0:T(8,128)} %param.4) | copy-start | bytes 786436
  28.7 16.3 %all-to-all-start.1 = ((f32[3,8,64,128]{3,1,0,2:T(8,128)}), f32[3,8,64,128]{3,1,0,2:T(8,128)S(1)}, u32[]{:S(2)}, u32[]{:S(2)}) async-start(f32[3,8,64,128]{3,1,0,2:T(8,128)} %all_to_all.33), calls=%async_computation.1 | async-start | bytes 1572864 | tf_op jit(solution)/shard_map/all_to_all | solution.py:139
  45.3 4.6 %collective-permute-start = (f32[4,8,1,1024]{3,2,1,0:T(1,128)S(1)}, f32[4,8,1,1024]{3,2,1,0:T(1,128)S(1)}, u32[]{:S(2)}, u32[]{:S(2)}) collective-permute-start(f32[4,8,1,1024]{3,2,1,0:T(1,128)S(1)} %get-tuple-element.9), channel_id=1, source_target_pairs={{0,1},{1,2},{2,3},{3,4},{4,5},{5,6},{6,7},{7,8},{8,9},{9,10},{10,1... | collective-permute-start | bytes 393224 | tf_op jit(solution)/shard_map/ppermute | solution.py:20
  47.4 7.3 %collective-permute-start.1 = (f32[4,8,1,1024]{3,2,1,0:T(1,128)S(1)}, f32[4,8,1,1024]{3,2,1,0:T(1,128)S(1)}, u32[]{:S(2)}, u32[]{:S(2)}) collective-permute-start(f32[4,8,1,1024]{3,2,1,0:T(1,128)S(1)} %get-tuple-element.10), channel_id=1, source_target_pairs={{1,0},{2,1},{3,2},{4,3},{5,4},{6,5},{7,6},{8,7},{9,8},{10,9},{11,1... | collective-permute-start | bytes 393224 | tf_op jit(solution)/shard_map/ppermute | solution.py:22
  56.4 1.1 copy-start.1
  58.9 4.2 %collective-permute-start.2 = (f32[1,8,1,1024]{3,2,1,0:T(1,128)S(1)}, f32[1,8,1,1024]{3,2,1,0:T(1,128)S(1)}, u32[]{:S(2)}, u32[]{:S(2)}) collective-permute-start(f32[1,8,1,1024]{3,2,1,0:T(1,128)S(1)} %get-tuple-element.11), channel_id=1, source_target_pairs={{0,1},{1,2},{2,3},{3,4},{4,5},{5,6},{6,7},{7,8},{8,9},{9,10},{10,1... | collective-permute-start | bytes 98312 | tf_op jit(solution)/shard_map/ppermute | solution.py:20
  61.4 6.3 %collective-permute-start.3 = (f32[1,8,1,1024]{3,2,1,0:T(1,128)S(1)}, f32[1,8,1,1024]{3,2,1,0:T(1,128)S(1)}, u32[]{:S(2)}, u32[]{:S(2)}) collective-permute-start(f32[1,8,1,1024]{3,2,1,0:T(1,128)S(1)} %get-tuple-element.12), channel_id=1, source_target_pairs={{1,0},{2,1},{3,2},{4,3},{5,4},{6,5},{7,6},{8,7},{9,8},{10,9},{11,1... | collective-permute-start | bytes 98312 | tf_op jit(solution)/shard_map/ppermute | solution.py:22
  68.6 5.5 %collective-permute-start.4 = (f32[8,1,1024]{2,1,0:T(1,128)S(1)}, f32[8,1,1024]{2,1,0:T(1,128)S(1)}, u32[]{:S(2)}, u32[]{:S(2)}) collective-permute-start(f32[8,1,1024]{2,1,0:T(1,128)S(1)} %get-tuple-element.37), channel_id=1, source_target_pairs={{0,1},{1,2},{2,3},{3,4},{4,5},{5,6},{6,7},{7,8},{8,9},{9,10},{10,1... | collective-permute-start | bytes 98312 | tf_op jit(solution)/shard_map/ppermute | solution.py:20
  72.5 5.8 %collective-permute-start.5 = (f32[8,1,1024]{2,1,0:T(1,128)S(1)}, f32[8,1,1024]{2,1,0:T(1,128)S(1)}, u32[]{:S(2)}, u32[]{:S(2)}) collective-permute-start(f32[8,1,1024]{2,1,0:T(1,128)S(1)} %get-tuple-element.38), channel_id=1, source_target_pairs={{1,0},{2,1},{3,2},{4,3},{5,4},{6,5},{7,6},{8,7},{9,8},{10,9},{11,1... | collective-permute-start | bytes 98312 | tf_op jit(solution)/shard_map/ppermute | solution.py:22
  79.2 3.8 %collective-permute-start.6 = (f32[8,1,1024]{2,1,0:T(1,128)S(1)}, f32[8,1,1024]{2,1,0:T(1,128)S(1)}, u32[]{:S(2)}, u32[]{:S(2)}) collective-permute-start(f32[8,1,1024]{2,1,0:T(1,128)S(1)} %get-tuple-element.35), channel_id=1, source_target_pairs={{0,1},{1,2},{2,3},{3,4},{4,5},{5,6},{6,7},{7,8},{8,9},{9,10},{10,1... | collective-permute-start | bytes 98312 | tf_op jit(solution)/shard_map/ppermute | solution.py:20
  81.4 5.8 %collective-permute-start.7 = (f32[8,1,1024]{2,1,0:T(1,128)S(1)}, f32[8,1,1024]{2,1,0:T(1,128)S(1)}, u32[]{:S(2)}, u32[]{:S(2)}) collective-permute-start(f32[8,1,1024]{2,1,0:T(1,128)S(1)} %get-tuple-element.36), channel_id=1, source_target_pairs={{1,0},{2,1},{3,2},{4,3},{5,4},{6,5},{7,6},{8,7},{9,8},{10,9},{11,1... | collective-permute-start | bytes 98312 | tf_op jit(solution)/shard_map/ppermute | solution.py:22
  88.1 4.5 %collective-permute-start.8 = (f32[8,1,1024]{2,1,0:T(1,128)S(1)}, f32[8,1,1024]{2,1,0:T(1,128)S(1)}, u32[]{:S(2)}, u32[]{:S(2)}) collective-permute-start(f32[8,1,1024]{2,1,0:T(1,128)S(1)} %get-tuple-element.33), channel_id=1, source_target_pairs={{0,1},{1,2},{2,3},{3,4},{4,5},{5,6},{6,7},{7,8},{8,9},{9,10},{10,1... | collective-permute-start | bytes 98312 | tf_op jit(solution)/shard_map/ppermute | solution.py:20
  91.0 5.8 %collective-permute-start.9 = (f32[8,1,1024]{2,1,0:T(1,128)S(1)}, f32[8,1,1024]{2,1,0:T(1,128)S(1)}, u32[]{:S(2)}, u32[]{:S(2)}) collective-permute-start(f32[8,1,1024]{2,1,0:T(1,128)S(1)} %get-tuple-element.34), channel_id=1, source_target_pairs={{1,0},{2,1},{3,2},{4,3},{5,4},{6,5},{7,6},{8,7},{9,8},{10,9},{11,1... | collective-permute-start | bytes 98312 | tf_op jit(solution)/shard_map/ppermute | solution.py:22
  97.7 5.7 %collective-permute-start.10 = (f32[8,1,1024]{2,1,0:T(1,128)S(1)}, f32[8,1,1024]{2,1,0:T(1,128)S(1)}, u32[]{:S(2)}, u32[]{:S(2)}) collective-permute-start(f32[8,1,1024]{2,1,0:T(1,128)S(1)} %get-tuple-element.31), channel_id=1, source_target_pairs={{0,1},{1,2},{2,3},{3,4},{4,5},{5,6},{6,7},{7,8},{8,9},{9,10},{10,1... | collective-permute-start | bytes 98312 | tf_op jit(solution)/shard_map/ppermute | solution.py:20
  101.8 6.2 %collective-permute-start.11 = (f32[8,1,1024]{2,1,0:T(1,128)S(1)}, f32[8,1,1024]{2,1,0:T(1,128)S(1)}, u32[]{:S(2)}, u32[]{:S(2)}) collective-permute-start(f32[8,1,1024]{2,1,0:T(1,128)S(1)} %get-tuple-element.32), channel_id=1, source_target_pairs={{1,0},{2,1},{3,2},{4,3},{5,4},{6,5},{7,6},{8,7},{9,8},{10,9},{11,1... | collective-permute-start | bytes 98312 | tf_op jit(solution)/shard_map/ppermute | solution.py:22
  108.9 5.5 %collective-permute-start.12 = (f32[8,1,1024]{2,1,0:T(1,128)S(1)}, f32[8,1,1024]{2,1,0:T(1,128)S(1)}, u32[]{:S(2)}, u32[]{:S(2)}) collective-permute-start(f32[8,1,1024]{2,1,0:T(1,128)S(1)} %get-tuple-element.29), channel_id=1, source_target_pairs={{0,1},{1,2},{2,3},{3,4},{4,5},{5,6},{6,7},{7,8},{8,9},{9,10},{10,1... | collective-permute-start | bytes 98312 | tf_op jit(solution)/shard_map/ppermute | solution.py:20
  112.8 6.1 %collective-permute-start.13 = (f32[8,1,1024]{2,1,0:T(1,128)S(1)}, f32[8,1,1024]{2,1,0:T(1,128)S(1)}, u32[]{:S(2)}, u32[]{:S(2)}) collective-permute-start(f32[8,1,1024]{2,1,0:T(1,128)S(1)} %get-tuple-element.30), channel_id=1, source_target_pairs={{1,0},{2,1},{3,2},{4,3},{5,4},{6,5},{7,6},{8,7},{9,8},{10,9},{11,1... | collective-permute-start | bytes 98312 | tf_op jit(solution)/shard_map/ppermute | solution.py:22
  119.8 5.3 %collective-permute-start.14 = (f32[8,1,1024]{2,1,0:T(1,128)S(1)}, f32[8,1,1024]{2,1,0:T(1,128)S(1)}, u32[]{:S(2)}, u32[]{:S(2)}) collective-permute-start(f32[8,1,1024]{2,1,0:T(1,128)S(1)} %get-tuple-element.27), channel_id=1, source_target_pairs={{0,1},{1,2},{2,3},{3,4},{4,5},{5,6},{6,7},{7,8},{8,9},{9,10},{10,1... | collective-permute-start | bytes 98312 | tf_op jit(solution)/shard_map/ppermute | solution.py:20
  123.6 6.1 %collective-permute-start.15 = (f32[8,1,1024]{2,1,0:T(1,128)S(1)}, f32[8,1,1024]{2,1,0:T(1,128)S(1)}, u32[]{:S(2)}, u32[]{:S(2)}) collective-permute-start(f32[8,1,1024]{2,1,0:T(1,128)S(1)} %get-tuple-element.28), channel_id=1, source_target_pairs={{1,0},{2,1},{3,2},{4,3},{5,4},{6,5},{7,6},{8,7},{9,8},{10,9},{11,1... | collective-permute-start | bytes 98312 | tf_op jit(solution)/shard_map/ppermute | solution.py:22
  130.6 5.3 %collective-permute-start.16 = (f32[8,1,1024]{2,1,0:T(1,128)S(1)}, f32[8,1,1024]{2,1,0:T(1,128)S(1)}, u32[]{:S(2)}, u32[]{:S(2)}) collective-permute-start(f32[8,1,1024]{2,1,0:T(1,128)S(1)} %get-tuple-element.25), channel_id=1, source_target_pairs={{0,1},{1,2},{2,3},{3,4},{4,5},{5,6},{6,7},{7,8},{8,9},{9,10},{10,1... | collective-permute-start | bytes 98312 | tf_op jit(solution)/shard_map/ppermute | solution.py:20
  134.3 6.1 %collective-permute-start.17 = (f32[8,1,1024]{2,1,0:T(1,128)S(1)}, f32[8,1,1024]{2,1,0:T(1,128)S(1)}, u32[]{:S(2)}, u32[]{:S(2)}) collective-permute-start(f32[8,1,1024]{2,1,0:T(1,128)S(1)} %get-tuple-element.26), channel_id=1, source_target_pairs={{1,0},{2,1},{3,2},{4,3},{5,4},{6,5},{7,6},{8,7},{9,8},{10,9},{11,1... | collective-permute-start | bytes 98312 | tf_op jit(solution)/shard_map/ppermute | solution.py:22
  141.3 29.5 %collective-permute-start.19 = (f32[8,1,1024]{2,1,0:T(1,128)S(1)}, f32[8,1,1024]{2,1,0:T(1,128)S(1)}, u32[]{:S(2)}, u32[]{:S(2)}) collective-permute-start(f32[8,1,1024]{2,1,0:T(1,128)S(1)} %get-tuple-element.23), channel_id=1, source_target_pairs={{0,1},{1,2},{2,3},{3,4},{4,5},{5,6},{6,7},{7,8},{8,9},{9,10},{10,1... | collective-permute-start | bytes 98312 | tf_op jit(solution)/shard_map/ppermute | solution.py:20
  145.0 25.8 %collective-permute-start.18 = (f32[8,1,1024]{2,1,0:T(1,128)S(1)}, f32[8,1,1024]{2,1,0:T(1,128)S(1)}, u32[]{:S(2)}, u32[]{:S(2)}) collective-permute-start(f32[8,1,1024]{2,1,0:T(1,128)S(1)} %get-tuple-element.24), channel_id=1, source_target_pairs={{1,0},{2,1},{3,2},{4,3},{5,4},{6,5},{7,6},{8,7},{9,8},{10,9},{11,1... | collective-permute-start | bytes 98312 | tf_op jit(solution)/shard_map/ppermute | solution.py:22
  151.3 26.4 %all-to-all-start.2 = ((f32[8,1,8,8,128]{4,3,2,1,0:T(8,128)}), f32[8,1,8,8,128]{4,3,2,1,0:T(8,128)S(1)}, u32[]{:S(2)}, u32[]{:S(2)}) async-start(f32[8,1,8,8,128]{4,3,2,1,0:T(8,128)} %fusion.122), calls=%async_computation.2 | async-start | bytes 524288 | tf_op jit(solution)/shard_map/all_to_all | solution.py:126
  178.6 12.0 %all-to-all-start.3 = ((f32[1,8,64,128]{3,1,0,2:T(8,128)}), f32[1,8,64,128]{3,1,0,2:T(8,128)S(1)}, u32[]{:S(2)}, u32[]{:S(2)}) async-start(f32[1,8,64,128]{3,1,0,2:T(8,128)} %copy.27), calls=%async_computation.3 | async-start | bytes 524288 | tf_op jit(solution)/shard_map/all_to_all | solution.py:124
